TPU v7x, 32 devices: a whole 2x2x4 slice. The times are simulated.
32 devices in a mesh: look: 16 (over z, y, core), swath: 2 (over x).
Axes of the slice: x: 2, y: 2, z: 4, core: 2. Of those that a mesh axis runs over, the one named last changes fastest.
Arguments:
- images: bfloat16 [32, 8, 2, 512, 512], P('look', 'swath'), may hold values from -6 to 6
- patch_weight: float32 [8], P('swath'), may hold values from 1 to 10
- pair_mask: int32 [32, 4], P('look'), may hold values 0 or 1
Outputs:
- drift: float32 [32, 4, 256, 256], P('look', None, 'swath')
All inputs are finite; a program needn't handle non-finite values. No bound on the sum of `pair_mask` on one device may be relied on, other than what follows from the above.
Results may differ from a plain program's by a relative error of at most 0.015.
Values may be sent and summed in bfloat16 or wider, within the bound.
A program may use at most 128 MiB of HBM per device.

v0:
```python
import functools
import math

import jax
import jax.numpy as jnp
import numpy as np
from jax import lax
from jax.experimental import pallas as pl
from jax.experimental.pallas import tpu as pltpu
from jax.sharding import PartitionSpec as P

PIX = 512
BAND = 256
WIN = 256
HALF = PIX // 2


def phases(rows, cols, row_shift, col_shift):
    phase = (rows[:, None] - row_shift) * (cols[None, :] - col_shift) % PIX
    angle = 2.0 * math.pi / PIX * phase
    return np.cos(angle), np.sin(angle)


def forward_tables():
    left, right = [], []
    for parity in (0, 1):
        re, im = phases(np.arange(parity, BAND, 2), np.arange(HALF), BAND // 2, 0)
        im = -im
        left.append(np.block([[re, -im], [im, re]]))
        right.append(np.block([[re.T, im.T], [-im.T, re.T]]))
    return jnp.asarray(np.stack(left), jnp.bfloat16), jnp.asarray(np.stack(right), jnp.bfloat16)


def inverse_tables():
    order = np.concatenate([np.arange(0, BAND, 2), np.arange(1, BAND, 2)])
    re, im = phases(np.arange(WIN), order, WIN // 2, BAND // 2)
    first = np.concatenate([re, im], axis=0)
    second = np.stack([re.T, im.T])
    return jnp.asarray(first, jnp.bfloat16), jnp.asarray(second, jnp.bfloat16)


def dot(left, right):
    return jnp.dot(left, right, preferred_element_type=jnp.float32)


ROWS = 32
MESH = pl.DeviceIdType.MESH


def spectrum_of(img, left_ref, right_ref):
    re0, re1 = img[0, :HALF, :], img[0, HALF:, :]
    im0, im1 = img[1, :HALF, :], img[1, HALF:, :]
    even = dot(left_ref[0], jnp.concatenate([re0 + re1, im0 + im1], axis=0))
    odd = dot(left_ref[1], jnp.concatenate([re0 - re1, im0 - im1], axis=0))
    quarter = BAND // 2
    parts = []
    for at in (0, quarter):
        parts.append(jnp.concatenate([even[at : at + quarter], odd[at : at + quarter]], axis=0))
    plus = [(part[:, :HALF] + part[:, HALF:]).astype(jnp.bfloat16) for part in parts]
    minus = [(part[:, :HALF] - part[:, HALF:]).astype(jnp.bfloat16) for part in parts]
    spec_even = dot(jnp.concatenate(plus, axis=1), right_ref[0]).astype(jnp.bfloat16)
    spec_odd = dot(jnp.concatenate(minus, axis=1), right_ref[1]).astype(jnp.bfloat16)
    return spec_even, spec_odd


def squares_of(spec_even, spec_odd):
    total = spec_even.astype(jnp.float32) ** 2 + spec_odd.astype(jnp.float32) ** 2
    folded = jnp.sum(total.reshape(BAND // 8, 8, BAND), axis=0)
    return folded[:, : BAND // 2] + folded[:, BAND // 2 :]


def cross_into(w_ref, a_ref, b_ref, cre, cim):
    patches = a_ref.shape[0]

    def step(i, carry):
        rows = pl.ds(pl.multiple_of(i * ROWS, ROWS), ROWS)
        re = jnp.zeros((ROWS, BAND), jnp.float32)
        im = jnp.zeros((ROWS, BAND), jnp.float32)
        for p in range(patches):
            weight = w_ref[p]
            ar = a_ref[p, 0, rows, :].astype(jnp.float32) * weight
            ai = a_ref[p, 1, rows, :].astype(jnp.float32) * weight
            br = b_ref[p, 0, rows, :].astype(jnp.float32)
            bi = b_ref[p, 1, rows, :].astype(jnp.float32)
            re += ar * br + ai * bi
            im += ai * br - ar * bi
        cre[rows, :] = re.astype(jnp.bfloat16)
        cim[rows, :] = im.astype(jnp.bfloat16)
        return carry

    lax.fori_loop(0, BAND // ROWS, step, 0)


def halves(first_ref, second_ref, cre, cim):
    from_re = dot(first_ref[...], cre[...]).astype(jnp.bfloat16)
    from_im = dot(first_ref[...], cim[...]).astype(jnp.bfloat16)
    keep = dot(from_re[:WIN], second_ref[0]) - dot(from_re[WIN:], second_ref[1])
    turn = dot(from_im[:WIN], second_ref[1]) + dot(from_im[WIN:], second_ref[0])
    return keep, turn


PAIRS = 7


def kernel(nlook, nswath, w_ref, mask_ref, img_ref, left_ref, right_ref, first_ref, second_ref, out_ref,
           img, own, near, far, opp, energy, heard, cre, cim, surf, outbox, inbox, backbox,
           img_sem, near_send, near_recv, far_send, far_recv, opp_send, opp_recv,
           heard_send, heard_recv, box_send, box_recv, back_send, back_recv):
    looks, patches = img_ref.shape[:2]
    half = nlook // 2
    me, lane = lax.axis_index("look"), lax.axis_index("swath")
    odd = lax.rem(me, 2) == 1
    low = me < half
    sent_look = jnp.where(low, 1, 0)
    kept_look = 1 - sent_look

    def device(look_by, swath_by=0):
        return (lax.rem(me + look_by + nlook, nlook), lax.rem(lane + swath_by, nswath))

    def load(u):
        return pltpu.make_async_copy(img_ref.at[u // patches, u % patches], img.at[u], img_sem.at[u])

    for u in range(looks * patches):
        load(u).start()

    barrier = pltpu.get_barrier_semaphore()
    greeted = 0
    for look_by in (0, 1, -1, 2, -2, half):
        for by in range(nswath):
            if look_by or by:
                greeted += 1
                pl.semaphore_signal(barrier, inc=1, device_id=device(look_by, by), device_id_type=MESH)
    pl.semaphore_wait(barrier, greeted)

    def remote(src, dst, send, recv, to):
        return pltpu.make_async_remote_copy(
            src_ref=src, dst_ref=dst, send_sem=send, recv_sem=recv, device_id=to, device_id_type=MESH
        )

    def to_near(look, p):
        at = look * patches + p
        return remote(own.at[look, p], near.at[look, p], near_send.at[at], near_recv.at[at], device(-1))

    def to_opp(p):
        return remote(own.at[sent_look, p], opp.at[p], opp_send.at[p], opp_recv.at[p], device(half))

    def to_far(p):
        return remote(own.at[0, p], far.at[p], far_send.at[p], far_recv.at[p], device(-2))

    def relay(p):
        sem = far_send.at[patches + p]
        return remote(near.at[0, p], far.at[p], sem, far_recv.at[p], device(-1))

    def send(look, p):
        to_near(look, p).start()

        @pl.when(jnp.logical_and(odd, look == 0))
        def _():
            to_far(p).start()

        @pl.when(look == sent_look)
        def _():
            to_opp(p).start()

    for look in range(looks):
        energy[look] = jnp.zeros((8, 128), jnp.float32)

    def forward(u, carry):
        look, p = u // patches, u % patches
        load_u = pltpu.make_async_copy(img_ref.at[look, p], img.at[u], img_sem.at[u])
        load_u.wait()
        spec_even, spec_odd = spectrum_of(img.at[u], left_ref, right_ref)
        quarter = BAND // 2
        own[look, p, 0, :, :quarter] = spec_even[:, :quarter]
        own[look, p, 0, :, quarter:] = spec_odd[:, :quarter]
        own[look, p, 1, :, :quarter] = spec_even[:, quarter:]
        own[look, p, 1, :, quarter:] = spec_odd[:, quarter:]
        energy[look] += w_ref[p] * squares_of(spec_even, spec_odd)

        @pl.when(u > 0)
        def _():
            send((u - 1) // patches, (u - 1) % patches)

        return carry

    lax.fori_loop(0, looks * patches, forward, 0)
    send(looks - 1, patches - 1)

    tell = []
    for d, look_by in enumerate((0, 1, 2, half)):
        for by in range(nswath):
            if look_by or by:
                tell.append(remote(energy, heard.at[d, by], heard_send.at[d, by], heard_recv.at[d, by],
                                   device(-look_by, by)))
    for copy in tell:
        copy.start()

    rows = WIN // nswath
    mine = pl.ds(pl.multiple_of(lane * rows, rows), rows)

    def outgoing(slot, by):
        at = pl.ds(pl.multiple_of(lax.rem(lane + by, nswath) * rows, rows), rows)
        return remote(outbox.at[slot, at], inbox.at[by - 1, slot], box_send.at[by - 1, slot],
                      box_recv.at[by - 1, slot], device(0, by))

    def returned(by):
        at = pl.ds(pl.multiple_of(lax.rem(lane + by, nswath) * rows, rows), rows)
        return remote(outbox.at[PAIRS, at], backbox.at[by], back_send.at[by], back_recv.at[by],
                      device(half, by))

    def pair(slot, a, b_ref):
        cross_into(w_ref, own.at[a], b_ref, cre, cim)
        keep, turn = halves(first_ref, second_ref, cre, cim)
        value = keep - turn
        surf[slot] = value
        outbox[slot] = value.astype(jnp.bfloat16)
        if slot == PAIRS - 1:
            outbox[PAIRS] = (keep + turn).astype(jnp.bfloat16)
            for by in range(nswath):
                returned(by).start()
        for by in range(1, nswath):
            outgoing(slot, by).start()

    pair(0, 0, own.at[1])
    for p in range(patches):
        to_near(0, p).wait_recv()

        @pl.when(odd)
        def _():
            relay(p).start()

    pair(1, 0, near.at[0])
    pair(3, 1, near.at[0])
    for p in range(patches):
        to_near(1, p).wait_recv()
    pair(2, 0, near.at[1])
    pair(4, 1, near.at[1])
    for p in range(patches):
        to_far(p).wait_recv()
    pair(5, 1, far)
    for p in range(patches):
        to_opp(p).wait_recv()
    pair(6, kept_look, opp)

    for copy in tell:
        copy.wait_recv()
    total = []
    for d in range(4):
        for look in range(looks):
            parts = energy[look] if d == 0 else heard[d, 0, look]
            for by in range(1, nswath):
                parts = parts + heard[d, by, look]
            total.append(jnp.sum(parts, axis=(0, 1), keepdims=True))
    scale = BAND * math.sqrt(patches * nswath)

    def factor(look, lag):
        mate = total[look + lag + 1] if lag < 3 else total[3 * looks + look]
        return mask_ref[look, lag].astype(jnp.float32) * scale / jnp.sqrt(total[look] * mate)

    def summed(slot):
        value = surf[slot, mine, :]
        for by in range(1, nswath):
            outgoing(slot, by).wait_recv()
            value = value + inbox[by - 1, slot].astype(jnp.float32)
        return value

    for slot in range(PAIRS - 1):
        out_ref[slot // 3, slot % 3] = summed(slot) * factor(slot // 3, slot % 3)
    kept = summed(PAIRS - 1)
    back = jnp.zeros((rows, WIN), jnp.float32)
    for by in range(nswath):
        returned(by).wait_recv()
        back = back + backbox[by].astype(jnp.float32)
    out_ref[0, 3] = jnp.where(low, kept, back) * factor(0, 3)
    out_ref[1, 3] = jnp.where(low, back, kept) * factor(1, 3)

    for look in range(looks):
        for p in range(patches):
            to_near(look, p).wait_send()
    for p in range(patches):
        to_opp(p).wait_send()

        @pl.when(odd)
        def _():
            to_far(p).wait_send()
            relay(p).wait_send()

    for copy in tell:
        copy.wait_send()
    for by in range(nswath):
        returned(by).wait_send()
    for slot in range(PAIRS):
        for by in range(1, nswath):
            outgoing(slot, by).wait_send()


def per_device(images, patch_weight, pair_mask):
    nlook = lax.axis_size("look")
    nswath = lax.axis_size("swath")
    looks, patches = images.shape[:2]
    left, right = forward_tables()
    first, second = inverse_tables()
    rows = WIN // nswath
    vmem = pl.BlockSpec(memory_space=pltpu.VMEM)
    smem = pl.BlockSpec(memory_space=pltpu.SMEM)
    dma = pltpu.SemaphoreType.DMA
    unit = (2, BAND, BAND)
    others = max(nswath - 1, 1)
    return pl.pallas_call(
        functools.partial(kernel, nlook, nswath),
        in_specs=[smem, smem, pl.BlockSpec(memory_space=pl.ANY)] + [vmem] * 4,
        out_specs=vmem,
        out_shape=jax.ShapeDtypeStruct((looks, 4, rows, WIN), jnp.float32),
        scratch_shapes=[
            pltpu.VMEM((looks * patches, 2, PIX, PIX), jnp.bfloat16),
            pltpu.VMEM((looks, patches) + unit, jnp.bfloat16),
            pltpu.VMEM((looks, patches) + unit, jnp.bfloat16),
            pltpu.VMEM((patches,) + unit, jnp.bfloat16),
            pltpu.VMEM((patches,) + unit, jnp.bfloat16),
            pltpu.VMEM((looks, 8, 128), jnp.float32),
            pltpu.VMEM((4, nswath, looks, 8, 128), jnp.float32),
            pltpu.VMEM((BAND, BAND), jnp.bfloat16),
            pltpu.VMEM((BAND, BAND), jnp.bfloat16),
            pltpu.VMEM((PAIRS, WIN, WIN), jnp.float32),
            pltpu.VMEM((PAIRS + 1, WIN, WIN), jnp.bfloat16),
            pltpu.VMEM((others, PAIRS, rows, WIN), jnp.bfloat16),
            pltpu.VMEM((nswath, rows, WIN), jnp.bfloat16),
            dma((looks * patches,)),
            dma((looks * patches,)),
            dma((looks * patches,)),
            dma((2 * patches,)),
            dma((patches,)),
            dma((patches,)),
            dma((patches,)),
            dma((4, nswath)),
            dma((4, nswath)),
            dma((others, PAIRS)),
            dma((others, PAIRS)),
            dma((nswath,)),
            dma((nswath,)),
        ],
        compiler_params=pltpu.CompilerParams(
            collective_id=0, has_side_effects=True, vmem_limit_bytes=48 * 2**20
        ),
        name="autofocus",
    )(patch_weight, pair_mask, images, left, right, first, second)


def solution(mesh):
    return jax.shard_map(
        per_device,
        mesh=mesh,
        in_specs=(P("look", "swath", None, None, None), P("swath"), P("look", None)),
        out_specs=P("look", None, "swath", None),
        check_vma=False,
    )
```

profile of v0, /device:TPU:8, one launch (start us, length us, event | category | flops | bytes accessed | tf_op | source)
XLA Modules:
  0.0 104.7 jit_solution(14055978569912055632)
XLA Ops:
  0.0 0.0 copy-start
  0.0 1.0 copy-done
  1.0 0.0 copy-start.1
  1.0 1.0 copy-done.1
  2.1 0.0 copy-start.2
  2.1 0.9 copy-done.2
  3.0 0.0 copy-start.3
  3.0 0.9 copy-done.3
  4.0 0.0 copy-start.4
  4.0 0.7 copy-done.4
  4.7 0.0 copy-start.5
  4.7 0.7 copy-done.5
  5.3 98.4 %autofocus.1 = f32[2,4,128,256]{3,2,1,0:T(8,128)S(1)} custom-call(f32[4]{0:T(128)S(1)} %copy-done.5, s32[2,4]{1,0:T(2,128)S(1)} %copy-done.4, bf16[2,4,2,512,512]{4,3,2,1,0:T(8,128)(2,1)} %img_ref.1, bf16[2,256,512]{2,1,0:T(8,128)(2,1)S(1)} %copy-done.1, bf16[2,512,256]{2,1,0:T(8,128)(2,1)S(1)} %copy-done, bf16[512,256]{1,0:T(8,128)(2,1)S(1)} %copy-done.3, ...), custom_call_target="tpu_custom_call" | custom-call | tf_op jit(solution)/shard_map/autofocus/pallas_call | solution.py:309
  103.8 1.0 copy.9
Async XLA Ops:
  0.0 1.0 copy-start
  1.0 1.0 copy-start.1
  2.1 0.9 copy-start.2
  3.0 0.9 copy-start.3
  4.0 0.7 copy-start.4
  4.7 0.7 copy-start.5
where the time goes:
time: 105 us
  Pallas kernels  98.4 us (94%)
  local copies, waits for them, and re-layouts  6.29 us (6%)
    pallas_call x1, Pallas kernels, per_device(): pl.pallas_call(functools.partial(kernel, nlook, nswath), in_specs=[smem,...  98.4 us
    unnamed x13, local copies, waits for them, and re-layouts  6.29 us

commit v1 on v0

--- a/solution.py
+++ b/solution.py
@@ -102,14 +102,15 @@
 PAIRS = 7
 
 
-def kernel(nlook, nswath, w_ref, mask_ref, img_ref, left_ref, right_ref, first_ref, second_ref, out_ref,
-           img, own, near, far, opp, energy, heard, cre, cim, surf, outbox, inbox, backbox,
-           img_sem, near_send, near_recv, far_send, far_recv, opp_send, opp_recv,
+def kernel(nlook, nswath, w_ref, mask_ref, img_ref, left_hbm, right_hbm, first_hbm, second_hbm, out_ref,
+           left_ref, right_ref, first_ref, second_ref, img, hop, own, near, far, opp, energy, heard, cre, cim, surf, outbox, inbox, backbox,
+           table_sem, hop_send, hop_recv, onward_send, img_sem, near_send, near_recv, far_send, far_recv, opp_send, opp_recv,
            heard_send, heard_recv, box_send, box_recv, back_send, back_recv):
     looks, patches = img_ref.shape[:2]
     half = nlook // 2
     me, lane = lax.axis_index("look"), lax.axis_index("swath")
     odd = lax.rem(me, 2) == 1
+    crossing = lax.rem(me, 4) < 2
     low = me < half
     sent_look = jnp.where(low, 1, 0)
     kept_look = 1 - sent_look
@@ -120,8 +121,19 @@
     def load(u):
         return pltpu.make_async_copy(img_ref.at[u // patches, u % patches], img.at[u], img_sem.at[u])
 
-    for u in range(looks * patches):
+    tables = [
+        pltpu.make_async_copy(src, dst, table_sem.at[i])
+        for i, (src, dst) in enumerate(
+            ((left_hbm, left_ref), (right_hbm, right_ref), (first_hbm, first_ref), (second_hbm, second_ref))
+        )
+    ]
+    load(0).start()
+    tables[0].start()
+    tables[1].start()
+    for u in range(1, looks * patches):
         load(u).start()
+    tables[2].start()
+    tables[3].start()
 
     barrier = pltpu.get_barrier_semaphore()
     greeted = 0
@@ -130,6 +142,9 @@
             if look_by or by:
                 greeted += 1
                 pl.semaphore_signal(barrier, inc=1, device_id=device(look_by, by), device_id_type=MESH)
+    for look_by in (3, -3, 4, -4):
+        greeted += 1
+        pl.semaphore_signal(barrier, inc=1, device_id=device(look_by), device_id_type=MESH)
     pl.semaphore_wait(barrier, greeted)
 
     def remote(src, dst, send, recv, to):
@@ -151,16 +166,43 @@
         sem = far_send.at[patches + p]
         return remote(near.at[0, p], far.at[p], sem, far_recv.at[p], device(-1))
 
+    def to_hop(look, p):
+        slot = look * (patches // 2) + p // 2
+        return remote(own.at[look, p], hop.at[slot], hop_send.at[slot], hop_recv.at[slot], device(2))
+
+    def onward_near(look, p):
+        slot = look * (patches // 2) + p // 2
+        at = look * patches + p
+        return remote(hop.at[slot], near.at[look, p], onward_send.at[slot], near_recv.at[at], device(-3))
+
+    def onward_far(p):
+        slot = p // 2
+        return remote(hop.at[slot], far.at[p], onward_send.at[slot], far_recv.at[p], device(-4))
+
+    def each_route(look, p, act):
+        via = jnp.logical_and(crossing, p % 2 == 1)
+        via_near = jnp.logical_and(via, jnp.logical_not(odd))
+        has_far = jnp.logical_and(odd, look == 0)
+        via_far = jnp.logical_and(via, has_far)
+
+        @pl.when(look == sent_look)
+        def _():
+            act(to_opp(p))
+
+        @pl.when(jnp.logical_or(via_near, via_far))
+        def _():
+            act(to_hop(look, p))
+
+        @pl.when(jnp.logical_not(via_near))
+        def _():
+            act(to_near(look, p))
+
+        @pl.when(jnp.logical_and(has_far, jnp.logical_not(via)))
+        def _():
+            act(to_far(p))
+
     def send(look, p):
-        to_near(look, p).start()
-
-        @pl.when(jnp.logical_and(odd, look == 0))
-        def _():
-            to_far(p).start()
-
-        @pl.when(look == sent_look)
-        def _():
-            to_opp(p).start()
+        each_route(look, p, lambda copy: copy.start())
 
     for look in range(looks):
         energy[look] = jnp.zeros((8, 128), jnp.float32)
@@ -183,6 +225,8 @@
 
         return carry
 
+    tables[0].wait()
+    tables[1].wait()
     lax.fori_loop(0, looks * patches, forward, 0)
     send(looks - 1, patches - 1)
 
@@ -221,7 +265,27 @@
         for by in range(1, nswath):
             outgoing(slot, by).start()
 
+    tables[2].wait()
+    tables[3].wait()
     pair(0, 0, own.at[1])
+
+    @pl.when(jnp.logical_not(crossing))
+    def _():
+        for look in range(looks):
+            for p in range(1, patches, 2):
+
+                @pl.when(jnp.logical_not(odd))
+                def _():
+                    to_hop(look, p).wait_recv()
+                    onward_near(look, p).start()
+
+                if look == 0:
+
+                    @pl.when(odd)
+                    def _():
+                        to_hop(look, p).wait_recv()
+                        onward_far(p).start()
+
     for p in range(patches):
         to_near(0, p).wait_recv()
 
@@ -231,16 +295,6 @@
 
     pair(1, 0, near.at[0])
     pair(3, 1, near.at[0])
-    for p in range(patches):
-        to_near(1, p).wait_recv()
-    pair(2, 0, near.at[1])
-    pair(4, 1, near.at[1])
-    for p in range(patches):
-        to_far(p).wait_recv()
-    pair(5, 1, far)
-    for p in range(patches):
-        to_opp(p).wait_recv()
-    pair(6, kept_look, opp)
 
     for copy in tell:
         copy.wait_recv()
@@ -264,8 +318,25 @@
             value = value + inbox[by - 1, slot].astype(jnp.float32)
         return value
 
-    for slot in range(PAIRS - 1):
+    def finish(slot):
         out_ref[slot // 3, slot % 3] = summed(slot) * factor(slot // 3, slot % 3)
+
+    for p in range(patches):
+        to_far(p).wait_recv()
+    pair(5, 1, far)
+    finish(0)
+    finish(1)
+    finish(3)
+    for p in range(patches):
+        to_near(1, p).wait_recv()
+    pair(2, 0, near.at[1])
+    pair(4, 1, near.at[1])
+    finish(5)
+    for p in range(patches):
+        to_opp(p).wait_recv()
+    pair(6, kept_look, opp)
+    finish(2)
+    finish(4)
     kept = summed(PAIRS - 1)
     back = jnp.zeros((rows, WIN), jnp.float32)
     for by in range(nswath):
@@ -276,14 +347,27 @@
 
     for look in range(looks):
         for p in range(patches):
-            to_near(look, p).wait_send()
+            each_route(look, p, lambda copy: copy.wait_send())
     for p in range(patches):
-        to_opp(p).wait_send()
 
         @pl.when(odd)
         def _():
-            to_far(p).wait_send()
             relay(p).wait_send()
+
+    @pl.when(jnp.logical_not(crossing))
+    def _():
+        for look in range(looks):
+            for p in range(1, patches, 2):
+
+                @pl.when(jnp.logical_not(odd))
+                def _():
+                    onward_near(look, p).wait_send()
+
+                if look == 0:
+
+                    @pl.when(odd)
+                    def _():
+                        onward_far(p).wait_send()
 
     for copy in tell:
         copy.wait_send()
@@ -308,11 +392,16 @@
     others = max(nswath - 1, 1)
     return pl.pallas_call(
         functools.partial(kernel, nlook, nswath),
-        in_specs=[smem, smem, pl.BlockSpec(memory_space=pl.ANY)] + [vmem] * 4,
+        in_specs=[smem, smem] + [pl.BlockSpec(memory_space=pltpu.HBM)] * 5,
         out_specs=vmem,
         out_shape=jax.ShapeDtypeStruct((looks, 4, rows, WIN), jnp.float32),
         scratch_shapes=[
+            pltpu.VMEM(left.shape, jnp.bfloat16),
+            pltpu.VMEM(right.shape, jnp.bfloat16),
+            pltpu.VMEM(first.shape, jnp.bfloat16),
+            pltpu.VMEM(second.shape, jnp.bfloat16),
             pltpu.VMEM((looks * patches, 2, PIX, PIX), jnp.bfloat16),
+            pltpu.VMEM((looks * (patches // 2),) + unit, jnp.bfloat16),
             pltpu.VMEM((looks, patches) + unit, jnp.bfloat16),
             pltpu.VMEM((looks, patches) + unit, jnp.bfloat16),
             pltpu.VMEM((patches,) + unit, jnp.bfloat16),
@@ -325,6 +414,10 @@
             pltpu.VMEM((PAIRS + 1, WIN, WIN), jnp.bfloat16),
             pltpu.VMEM((others, PAIRS, rows, WIN), jnp.bfloat16),
             pltpu.VMEM((nswath, rows, WIN), jnp.bfloat16),
+            dma((4,)),
+            dma((looks * (patches // 2),)),
+            dma((looks * (patches // 2),)),
+            dma((looks * (patches // 2),)),
             dma((looks * patches,)),
             dma((looks * patches,)),
             dma((looks * patches,)),
@@ -340,7 +433,7 @@
             dma((nswath,)),
         ],
         compiler_params=pltpu.CompilerParams(
-            collective_id=0, has_side_effects=True, vmem_limit_bytes=48 * 2**20
+            collective_id=0, has_side_effects=True, vmem_limit_bytes=67043328
         ),
         name="autofocus",
     )(patch_weight, pair_mask, images, left, right, first, second)

time: 105 us -> 92 us (0.88)
  the two profiles are of different devices: /device:TPU:8 before, /device:TPU:12 now
where the time goes in v1:
time: 92 us; the launch traced here: 91.9 us
  Pallas kernels  89.6 us (97%)
  local copies, waits for them, and re-layouts  2.27 us (2%)
    pallas_call x1, Pallas kernels, per_device(): pl.pallas_call(functools.partial(kernel, nlook, nswath), in_specs=[smem,...  89.6 us
    unnamed x1, local copies, waits for them, and re-layouts  2.27 us

profile of v1, /device:TPU:12, one launch (start us, length us, event | category | flops | bytes accessed | tf_op | source)
XLA Modules:
  0.0 91.9 jit_solution(4490096244391874421)
XLA Ops:
  0.0 89.6 %autofocus.1 = f32[2,4,128,256]{3,2,1,0:T(8,128)} custom-call(f32[4]{0:T(128)} %w_ref.1, s32[2,4]{1,0:T(2,128)} %mask_ref.1, bf16[2,4,2,512,512]{4,3,2,1,0:T(8,128)(2,1)} %img_ref.1, bf16[2,256,512]{2,1,0:T(8,128)(2,1)} %constant.8.clone.left_hbm, bf16[2,512,256]{2,1,0:T(8,128)(2,1)} %constant.9.clone.right_hbm, bf16[512,256]{1,0:T(8,128)(2,1)} %constant.10.clone.first_hbm, ...), custom_call_target="tpu_custom_call" | custom-call | tf_op jit(solution)/shard_map/autofocus/pallas_call | solution.py:393
  89.6 2.3 %copy.9 = f32[2,4,128,256]{3,2,1,0:T(8,128)} copy(f32[2,4,128,256]{3,2,1,0:T(8,128)} %autofocus.1) | data formatting | bytes 2097152

commit v2 on v1

--- a/solution.py
+++ b/solution.py
@@ -102,7 +102,7 @@
 PAIRS = 7
 
 
-def kernel(nlook, nswath, w_ref, mask_ref, img_ref, left_hbm, right_hbm, first_hbm, second_hbm, out_ref,
+def kernel(nlook, nswath, w_ref, mask_ref, img_ref, left_hbm, right_hbm, first_hbm, second_hbm, out_ref, factor_ref,
            left_ref, right_ref, first_ref, second_ref, img, hop, own, near, far, opp, energy, heard, cre, cim, surf, outbox, inbox, backbox,
            table_sem, hop_send, hop_recv, onward_send, img_sem, near_send, near_recv, far_send, far_recv, opp_send, opp_recv,
            heard_send, heard_recv, box_send, box_recv, back_send, back_recv):
@@ -118,8 +118,11 @@
     def device(look_by, swath_by=0):
         return (lax.rem(me + look_by + nlook, nlook), lax.rem(lane + swath_by, nswath))
 
+    def look_at(u):
+        return jnp.where(u // patches == 0, sent_look, kept_look)
+
     def load(u):
-        return pltpu.make_async_copy(img_ref.at[u // patches, u % patches], img.at[u], img_sem.at[u])
+        return pltpu.make_async_copy(img_ref.at[look_at(u), u % patches], img.at[u], img_sem.at[u])
 
     tables = [
         pltpu.make_async_copy(src, dst, table_sem.at[i])
@@ -185,10 +188,6 @@
         has_far = jnp.logical_and(odd, look == 0)
         via_far = jnp.logical_and(via, has_far)
 
-        @pl.when(look == sent_look)
-        def _():
-            act(to_opp(p))
-
         @pl.when(jnp.logical_or(via_near, via_far))
         def _():
             act(to_hop(look, p))
@@ -201,16 +200,24 @@
         def _():
             act(to_far(p))
 
-    def send(look, p):
-        each_route(look, p, lambda copy: copy.start())
+    def send(u):
+        p = u % patches
+
+        @pl.when(u < patches)
+        def _():
+            to_opp(p).start()
+
+        @pl.when(u >= patches)
+        def _():
+            for look in range(looks):
+                each_route(look, p, lambda copy: copy.start())
 
     for look in range(looks):
         energy[look] = jnp.zeros((8, 128), jnp.float32)
 
     def forward(u, carry):
-        look, p = u // patches, u % patches
-        load_u = pltpu.make_async_copy(img_ref.at[look, p], img.at[u], img_sem.at[u])
-        load_u.wait()
+        look, p = look_at(u), u % patches
+        load(u).wait()
         spec_even, spec_odd = spectrum_of(img.at[u], left_ref, right_ref)
         quarter = BAND // 2
         own[look, p, 0, :, :quarter] = spec_even[:, :quarter]
@@ -221,14 +228,14 @@
 
         @pl.when(u > 0)
         def _():
-            send((u - 1) // patches, (u - 1) % patches)
+            send(u - 1)
 
         return carry
 
     tables[0].wait()
     tables[1].wait()
     lax.fori_loop(0, looks * patches, forward, 0)
-    send(looks - 1, patches - 1)
+    send(looks * patches - 1)
 
     tell = []
     for d, look_by in enumerate((0, 1, 2, half)):
@@ -287,6 +294,9 @@
                         onward_far(p).start()
 
     for p in range(patches):
+        to_opp(p).wait_recv()
+    pair(6, kept_look, opp)
+    for p in range(patches):
         to_near(0, p).wait_recv()
 
         @pl.when(odd)
@@ -319,36 +329,38 @@
         return value
 
     def finish(slot):
-        out_ref[slot // 3, slot % 3] = summed(slot) * factor(slot // 3, slot % 3)
-
-    for p in range(patches):
-        to_far(p).wait_recv()
-    pair(5, 1, far)
+        out_ref[slot // 3, slot % 3] = summed(slot)
+
+    for look in range(looks):
+        for lag in range(4):
+            at = look * 4 + lag
+            factor_ref[at : at + 1, :] = jnp.broadcast_to(factor(look, lag), (1, 128))
     finish(0)
-    finish(1)
-    finish(3)
     for p in range(patches):
         to_near(1, p).wait_recv()
     pair(2, 0, near.at[1])
     pair(4, 1, near.at[1])
-    finish(5)
+    finish(1)
+    finish(3)
     for p in range(patches):
-        to_opp(p).wait_recv()
-    pair(6, kept_look, opp)
-    finish(2)
-    finish(4)
+        to_far(p).wait_recv()
+    pair(5, 1, far)
     kept = summed(PAIRS - 1)
     back = jnp.zeros((rows, WIN), jnp.float32)
     for by in range(nswath):
         returned(by).wait_recv()
         back = back + backbox[by].astype(jnp.float32)
-    out_ref[0, 3] = jnp.where(low, kept, back) * factor(0, 3)
-    out_ref[1, 3] = jnp.where(low, back, kept) * factor(1, 3)
+    out_ref[0, 3] = jnp.where(low, kept, back)
+    out_ref[1, 3] = jnp.where(low, back, kept)
+    finish(2)
+    finish(4)
+    finish(5)
 
     for look in range(looks):
         for p in range(patches):
             each_route(look, p, lambda copy: copy.wait_send())
     for p in range(patches):
+        to_opp(p).wait_send()
 
         @pl.when(odd)
         def _():
@@ -390,11 +402,14 @@
     dma = pltpu.SemaphoreType.DMA
     unit = (2, BAND, BAND)
     others = max(nswath - 1, 1)
-    return pl.pallas_call(
+    surfaces, factors = pl.pallas_call(
         functools.partial(kernel, nlook, nswath),
         in_specs=[smem, smem] + [pl.BlockSpec(memory_space=pltpu.HBM)] * 5,
-        out_specs=vmem,
-        out_shape=jax.ShapeDtypeStruct((looks, 4, rows, WIN), jnp.float32),
+        out_specs=[vmem, vmem],
+        out_shape=[
+            jax.ShapeDtypeStruct((looks, 4, rows, WIN), jnp.float32),
+            jax.ShapeDtypeStruct((looks * 4, 128), jnp.float32),
+        ],
         scratch_shapes=[
             pltpu.VMEM(left.shape, jnp.bfloat16),
             pltpu.VMEM(right.shape, jnp.bfloat16),
@@ -437,6 +452,7 @@
         ),
         name="autofocus",
     )(patch_weight, pair_mask, images, left, right, first, second)
+    return surfaces * factors[:, 0].reshape(looks, 4)[:, :, None, None]
 
 
 def solution(mesh):

time: 92 us -> 90 us (0.978)
  the two profiles are of different devices: /device:TPU:12 before, /device:TPU:24 now
where the time goes in v2:
time: 90 us; the launch traced here: 89.8 us
  Pallas kernels  86.6 us (96%)
  other arithmetic  2.36 us (3%)
    pallas_call x1, Pallas kernels, per_device(): pl.pallas_call(functools.partial(kernel, nlook, nswath), in_specs=[smem,...  86.6 us
    mul x1, other arithmetic, per_device(): return surfaces * factors[:, 0].reshape(looks, 4)[:, :, None, None]  2.36 us

profile of v2, /device:TPU:24, one launch (start us, length us, event | category | flops | bytes accessed | tf_op | source)
XLA Modules:
  0.0 89.8 jit_solution(11196348197966687816)
XLA Ops:
  0.0 86.6 %autofocus.1 = (f32[2,4,128,256]{3,2,1,0:T(8,128)}, f32[8,128]{1,0:T(8,128)}) custom-call(f32[4]{0:T(128)} %w_ref.1, s32[2,4]{1,0:T(2,128)} %mask_ref.1, bf16[2,4,2,512,512]{4,3,2,1,0:T(8,128)(2,1)} %img_ref.1, bf16[2,256,512]{2,1,0:T(8,128)(2,1)} %constant.8.clone.left_hbm, bf16[2,512,256]{2,1,0:T(8,128)(2,1)} %constant.9.clone.right_hbm, ...), custom_call_target="tpu_custom_call" | custom-call | tf_op jit(solution)/shard_map/autofocus/pallas_call | solution.py:405
  86.6 0.8 slice_reduce_fusion
  87.4 0.1 mul.10
  87.5 2.4 %broadcast_multiply_fusion = f32[2,4,128,256]{3,2,1,0:T(8,128)} fusion(f32[2,4,128,256]{3,2,1,0:T(8,128)} %get-tuple-element.7, f32[2,4]{1,0:T(2,128)S(1)} %mul.10), kind=kLoop, calls=%fused_computation | loop fusion | flops 262144 | bytes 2097184 | tf_op jit(solution)/shard_map/mul | solution.py:455

commit v3 on v2

--- a/solution.py
+++ b/solution.py
@@ -100,11 +100,12 @@
 
 
 PAIRS = 7
+LAST = PAIRS - 1
 
 
 def kernel(nlook, nswath, w_ref, mask_ref, img_ref, left_hbm, right_hbm, first_hbm, second_hbm, out_ref, factor_ref,
-           left_ref, right_ref, first_ref, second_ref, img, hop, own, near, far, opp, energy, heard, cre, cim, surf, outbox, inbox, backbox,
-           table_sem, hop_send, hop_recv, onward_send, img_sem, near_send, near_recv, far_send, far_recv, opp_send, opp_recv,
+           left_ref, right_ref, first_ref, second_ref, img, hop, own, near, far, opp, energy, heard, cre, cim, surf, outbox, inbox, turned, backbox,
+           table_sem, hop_send, hop_recv, onward_send, forward_send, img_sem, near_send, near_recv, far_send, far_recv, opp_send, opp_recv,
            heard_send, heard_recv, box_send, box_recv, back_send, back_recv):
     looks, patches = img_ref.shape[:2]
     half = nlook // 2
@@ -145,7 +146,7 @@
             if look_by or by:
                 greeted += 1
                 pl.semaphore_signal(barrier, inc=1, device_id=device(look_by, by), device_id_type=MESH)
-    for look_by in (3, -3, 4, -4):
+    for look_by in (3, -3, 4, -4, half - 1, 1 - half, half - 2, 2 - half):
         greeted += 1
         pl.semaphore_signal(barrier, inc=1, device_id=device(look_by), device_id_type=MESH)
     pl.semaphore_wait(barrier, greeted)
@@ -182,17 +183,51 @@
         slot = p // 2
         return remote(hop.at[slot], far.at[p], onward_send.at[slot], far_recv.at[p], device(-4))
 
+    def forwarded_near(source, look):
+        low_one = jnp.logical_and(source == 0, look == 1)
+        return jnp.logical_or(low_one, jnp.logical_and(source == half, look == 0))
+
+    def each_forward(p, act):
+        at = forward_send.at[p]
+
+        @pl.when(me == 0)
+        def _():
+            act(remote(opp.at[p], near.at[0, p], at, near_recv.at[p], device(half - 1)))
+
+        @pl.when(me == 1)
+        def _():
+            act(remote(opp.at[p], far.at[p], at, far_recv.at[p], device(half - 2)))
+
+        @pl.when(me == half)
+        def _():
+            act(remote(opp.at[p], near.at[1, p], at, near_recv.at[patches + p], device(half - 1)))
+
+    def each_onward(act):
+        for look in range(looks):
+            for p in range(1, patches, 2):
+
+                @pl.when(jnp.logical_not(jnp.logical_or(odd, forwarded_near(me - 2, look))))
+                def _():
+                    act(look, p, onward_near(look, p))
+
+                if look == 0:
+
+                    @pl.when(jnp.logical_and(odd, me != half + 3))
+                    def _():
+                        act(look, p, onward_far(p))
+
     def each_route(look, p, act):
         via = jnp.logical_and(crossing, p % 2 == 1)
-        via_near = jnp.logical_and(via, jnp.logical_not(odd))
-        has_far = jnp.logical_and(odd, look == 0)
+        has_near = jnp.logical_not(forwarded_near(me, look))
+        via_near = jnp.logical_and(jnp.logical_and(via, has_near), jnp.logical_not(odd))
+        has_far = jnp.logical_and(jnp.logical_and(odd, look == 0), me != half + 1)
         via_far = jnp.logical_and(via, has_far)
 
         @pl.when(jnp.logical_or(via_near, via_far))
         def _():
             act(to_hop(look, p))
 
-        @pl.when(jnp.logical_not(via_near))
+        @pl.when(jnp.logical_and(has_near, jnp.logical_not(via_near)))
         def _():
             act(to_near(look, p))
 
@@ -209,8 +244,11 @@
 
         @pl.when(u >= patches)
         def _():
-            for look in range(looks):
-                each_route(look, p, lambda copy: copy.start())
+            early = p < patches // 2
+            look = jnp.where(early, sent_look, kept_look)
+            for step in range(2):
+                patch = 2 * lax.rem(p, patches // 2) + step
+                each_route(look, patch, lambda copy: copy.start())
 
     for look in range(looks):
         energy[look] = jnp.zeros((8, 128), jnp.float32)
@@ -254,10 +292,8 @@
         return remote(outbox.at[slot, at], inbox.at[by - 1, slot], box_send.at[by - 1, slot],
                       box_recv.at[by - 1, slot], device(0, by))
 
-    def returned(by):
-        at = pl.ds(pl.multiple_of(lax.rem(lane + by, nswath) * rows, rows), rows)
-        return remote(outbox.at[PAIRS, at], backbox.at[by], back_send.at[by], back_recv.at[by],
-                      device(half, by))
+    def returned():
+        return remote(turned, backbox, back_send.at[0], back_recv.at[0], device(half))
 
     def pair(slot, a, b_ref):
         cross_into(w_ref, own.at[a], b_ref, cre, cim)
@@ -265,11 +301,14 @@
         value = keep - turn
         surf[slot] = value
         outbox[slot] = value.astype(jnp.bfloat16)
-        if slot == PAIRS - 1:
-            outbox[PAIRS] = (keep + turn).astype(jnp.bfloat16)
-            for by in range(nswath):
-                returned(by).start()
+        both = slot is LAST
+        if both:
+            value = keep + turn
+            surf[PAIRS] = value
+            outbox[PAIRS] = value.astype(jnp.bfloat16)
         for by in range(1, nswath):
+            if both:
+                outgoing(PAIRS, by).start()
             outgoing(slot, by).start()
 
     tables[2].wait()
@@ -278,33 +317,16 @@
 
     @pl.when(jnp.logical_not(crossing))
     def _():
-        for look in range(looks):
-            for p in range(1, patches, 2):
-
-                @pl.when(jnp.logical_not(odd))
-                def _():
-                    to_hop(look, p).wait_recv()
-                    onward_near(look, p).start()
-
-                if look == 0:
-
-                    @pl.when(odd)
-                    def _():
-                        to_hop(look, p).wait_recv()
-                        onward_far(p).start()
+        def onward(look, p, copy):
+            to_hop(look, p).wait_recv()
+            copy.start()
+
+        each_onward(onward)
 
     for p in range(patches):
         to_opp(p).wait_recv()
-    pair(6, kept_look, opp)
-    for p in range(patches):
-        to_near(0, p).wait_recv()
-
-        @pl.when(odd)
-        def _():
-            relay(p).start()
-
-    pair(1, 0, near.at[0])
-    pair(3, 1, near.at[0])
+        each_forward(p, lambda copy: copy.start())
+    pair(LAST, kept_look, opp)
 
     for copy in tell:
         copy.wait_recv()
@@ -331,25 +353,33 @@
     def finish(slot):
         out_ref[slot // 3, slot % 3] = summed(slot)
 
+    turned[...] = summed(PAIRS).astype(jnp.bfloat16)
     for look in range(looks):
         for lag in range(4):
             at = look * 4 + lag
             factor_ref[at : at + 1, :] = jnp.broadcast_to(factor(look, lag), (1, 128))
     finish(0)
-    for p in range(patches):
-        to_near(1, p).wait_recv()
-    pair(2, 0, near.at[1])
-    pair(4, 1, near.at[1])
-    finish(1)
-    finish(3)
+    returned().start()
+    ahead = lax.rem(me + 1, nlook)
+    first_look = jnp.where(ahead < half, 1, 0)
+    for look in (first_look, 1 - first_look):
+        for p in range(patches):
+            to_near(look, p).wait_recv()
+
+            @pl.when(jnp.logical_and(odd, look == 0))
+            def _():
+                relay(p).start()
+
+        pair(1 + look, 0, near.at[look])
+        pair(3 + look, 1, near.at[look])
     for p in range(patches):
         to_far(p).wait_recv()
     pair(5, 1, far)
+    finish(1)
+    finish(3)
     kept = summed(PAIRS - 1)
-    back = jnp.zeros((rows, WIN), jnp.float32)
-    for by in range(nswath):
-        returned(by).wait_recv()
-        back = back + backbox[by].astype(jnp.float32)
+    returned().wait_recv()
+    back = backbox[...].astype(jnp.float32)
     out_ref[0, 3] = jnp.where(low, kept, back)
     out_ref[1, 3] = jnp.where(low, back, kept)
     finish(2)
@@ -366,26 +396,16 @@
         def _():
             relay(p).wait_send()
 
+        each_forward(p, lambda copy: copy.wait_send())
+
     @pl.when(jnp.logical_not(crossing))
     def _():
-        for look in range(looks):
-            for p in range(1, patches, 2):
-
-                @pl.when(jnp.logical_not(odd))
-                def _():
-                    onward_near(look, p).wait_send()
-
-                if look == 0:
-
-                    @pl.when(odd)
-                    def _():
-                        onward_far(p).wait_send()
+        each_onward(lambda look, p, copy: copy.wait_send())
 
     for copy in tell:
         copy.wait_send()
-    for by in range(nswath):
-        returned(by).wait_send()
-    for slot in range(PAIRS):
+    returned().wait_send()
+    for slot in range(PAIRS + 1):
         for by in range(1, nswath):
             outgoing(slot, by).wait_send()
 
@@ -425,14 +445,16 @@
             pltpu.VMEM((4, nswath, looks, 8, 128), jnp.float32),
             pltpu.VMEM((BAND, BAND), jnp.bfloat16),
             pltpu.VMEM((BAND, BAND), jnp.bfloat16),
-            pltpu.VMEM((PAIRS, WIN, WIN), jnp.float32),
+            pltpu.VMEM((PAIRS + 1, WIN, WIN), jnp.float32),
             pltpu.VMEM((PAIRS + 1, WIN, WIN), jnp.bfloat16),
-            pltpu.VMEM((others, PAIRS, rows, WIN), jnp.bfloat16),
-            pltpu.VMEM((nswath, rows, WIN), jnp.bfloat16),
+            pltpu.VMEM((others, PAIRS + 1, rows, WIN), jnp.bfloat16),
+            pltpu.VMEM((rows, WIN), jnp.bfloat16),
+            pltpu.VMEM((rows, WIN), jnp.bfloat16),
             dma((4,)),
             dma((looks * (patches // 2),)),
             dma((looks * (patches // 2),)),
             dma((looks * (patches // 2),)),
+            dma((patches,)),
             dma((looks * patches,)),
             dma((looks * patches,)),
             dma((looks * patches,)),
@@ -442,10 +464,10 @@
             dma((patches,)),
             dma((4, nswath)),
             dma((4, nswath)),
-            dma((others, PAIRS)),
-            dma((others, PAIRS)),
-            dma((nswath,)),
-            dma((nswath,)),
+            dma((others, PAIRS + 1)),
+            dma((others, PAIRS + 1)),
+            dma((1,)),
+            dma((1,)),
         ],
         compiler_params=pltpu.CompilerParams(
             collective_id=0, has_side_effects=True, vmem_limit_bytes=67043328

time: 90 us -> 85.4 us (0.949)
  the two profiles are of different devices: /device:TPU:24 before, /device:TPU:13 now
where the time goes in v3:
time: 85.4 us; the launch traced here: 85.2 us
  Pallas kernels  81.9 us (96%)
  other arithmetic  2.36 us (3%)
  local copies, waits for them, and re-layouts  0.87 us (1%)
    pallas_call x1, Pallas kernels, per_device(): pl.pallas_call(functools.partial(kernel, nlook, nswath), in_specs=[smem,...  81.9 us
    mul x1, other arithmetic, per_device(): return surfaces * factors[:, 0].reshape(looks, 4)[:, :, None, None]  2.36 us

profile of v3, /device:TPU:13, one launch (start us, length us, event | category | flops | bytes accessed | tf_op | source)
XLA Modules:
  0.0 85.2 jit_solution(5033941703155664462)
XLA Ops:
  0.0 81.9 %autofocus.1 = (f32[2,4,128,256]{3,2,1,0:T(8,128)}, f32[8,128]{1,0:T(8,128)}) custom-call(f32[4]{0:T(128)} %w_ref.1, s32[2,4]{1,0:T(2,128)} %mask_ref.1, bf16[2,4,2,512,512]{4,3,2,1,0:T(8,128)(2,1)} %img_ref.1, bf16[2,256,512]{2,1,0:T(8,128)(2,1)} %constant.8.clone.left_hbm, bf16[2,512,256]{2,1,0:T(8,128)(2,1)} %constant.9.clone.right_hbm, ...), custom_call_target="tpu_custom_call" | custom-call | tf_op jit(solution)/shard_map/autofocus/pallas_call | solution.py:425
  81.9 0.8 slice_reduce_fusion
  82.7 0.1 mul.10
  82.8 2.4 %broadcast_multiply_fusion = f32[2,4,128,256]{3,2,1,0:T(8,128)} fusion(f32[2,4,128,256]{3,2,1,0:T(8,128)} %get-tuple-element.7, f32[2,4]{1,0:T(2,128)S(1)} %mul.10), kind=kLoop, calls=%fused_computation | loop fusion | flops 262144 | bytes 2097184 | tf_op jit(solution)/shard_map/mul | solution.py:477

commit v4 on v3

--- a/solution.py
+++ b/solution.py
@@ -323,6 +323,25 @@
 
         each_onward(onward)
 
+    late = jnp.logical_and(odd, jnp.logical_not(crossing))
+
+    def ring_pairs():
+        ahead = lax.rem(me + 1, nlook)
+        first_look = jnp.where(ahead < half, 1, 0)
+        for look in (first_look, 1 - first_look):
+            for p in range(patches):
+                to_near(look, p).wait_recv()
+
+                @pl.when(jnp.logical_and(odd, look == 0))
+                def _():
+                    relay(p).start()
+
+            pair(1 + look, 0, near.at[look])
+            pair(3 + look, 1, near.at[look])
+    @pl.when(jnp.logical_not(late))
+    def _():
+        ring_pairs()
+
     for p in range(patches):
         to_opp(p).wait_recv()
         each_forward(p, lambda copy: copy.start())
@@ -356,22 +375,14 @@
     turned[...] = summed(PAIRS).astype(jnp.bfloat16)
     for look in range(looks):
         for lag in range(4):
-            at = look * 4 + lag
-            factor_ref[at : at + 1, :] = jnp.broadcast_to(factor(look, lag), (1, 128))
+            factor_ref[look, lag] = jnp.broadcast_to(factor(look, lag), (1, WIN))
     finish(0)
     returned().start()
-    ahead = lax.rem(me + 1, nlook)
-    first_look = jnp.where(ahead < half, 1, 0)
-    for look in (first_look, 1 - first_look):
-        for p in range(patches):
-            to_near(look, p).wait_recv()
-
-            @pl.when(jnp.logical_and(odd, look == 0))
-            def _():
-                relay(p).start()
-
-        pair(1 + look, 0, near.at[look])
-        pair(3 + look, 1, near.at[look])
+
+    @pl.when(late)
+    def _():
+        ring_pairs()
+
     for p in range(patches):
         to_far(p).wait_recv()
     pair(5, 1, far)
@@ -428,7 +439,7 @@
         out_specs=[vmem, vmem],
         out_shape=[
             jax.ShapeDtypeStruct((looks, 4, rows, WIN), jnp.float32),
-            jax.ShapeDtypeStruct((looks * 4, 128), jnp.float32),
+            jax.ShapeDtypeStruct((looks, 4, 1, WIN), jnp.float32),
         ],
         scratch_shapes=[
             pltpu.VMEM(left.shape, jnp.bfloat16),
@@ -474,7 +485,7 @@
         ),
         name="autofocus",
     )(patch_weight, pair_mask, images, left, right, first, second)
-    return surfaces * factors[:, 0].reshape(looks, 4)[:, :, None, None]
+    return surfaces * factors
 
 
 def solution(mesh):

time: 85.4 us -> 82.3 us (0.964)
  Pallas kernels: 81.9 us -> 78.8 us
    pallas_call x1, Pallas kernels: 81.9 us -> 78.8 us  [per_device(): pl.pallas_call(functools.partial(kernel, nlook, nswath), in_specs=[smem,...]
where the time goes in v4:
time: 82.3 us; the launch traced here: 81.8 us
  Pallas kernels  78.8 us (96%)
  other arithmetic  2.29 us (3%)
    pallas_call x1, Pallas kernels, per_device(): pl.pallas_call(functools.partial(kernel, nlook, nswath), in_specs=[smem,...  78.8 us
    mul x1, other arithmetic, per_device(): return surfaces * factors  2.29 us

profile of v4, /device:TPU:13, one launch (start us, length us, event | category | flops | bytes accessed | tf_op | source)
XLA Modules:
  0.0 81.8 jit_solution(13038337657033797967)
XLA Ops:
  0.0 78.8 %autofocus.1 = (f32[2,4,128,256]{3,2,1,0:T(8,128)}, f32[2,4,1,256]{3,2,1,0:T(1,128)}) custom-call(f32[4]{0:T(128)} %w_ref.1, s32[2,4]{1,0:T(2,128)} %mask_ref.1, bf16[2,4,2,512,512]{4,3,2,1,0:T(8,128)(2,1)} %img_ref.1, bf16[2,256,512]{2,1,0:T(8,128)(2,1)} %constant.8.clone.left_hbm, bf16[2,512,256]{2,1,0:T(8,128)(2,1)} %constant.9.clone.right_hbm, ...), custom_call_target="tpu_custom_call" | custom-call | tf_op jit(solution)/shard_map/autofocus/pallas_call | solution.py:436
  78.8 0.7 copy.10
  79.5 2.3 %broadcast_multiply_fusion = f32[2,4,128,256]{3,2,1,0:T(8,128)} fusion(f32[2,4,128,256]{3,2,1,0:T(8,128)} %get-tuple-element.7, f32[2,4,256]{2,1,0:T(4,128)S(1)} %bitcast.3), kind=kLoop, calls=%fused_computation | loop fusion | flops 262144 | bytes 2105344 | tf_op jit(solution)/shard_map/mul | solution.py:488

commit v5 on v4

--- a/solution.py
+++ b/solution.py
@@ -254,6 +254,10 @@
         energy[look] = jnp.zeros((8, 128), jnp.float32)
 
     def forward(u, carry):
+        @pl.when(u > 0)
+        def _():
+            send(u - 1)
+
         look, p = look_at(u), u % patches
         load(u).wait()
         spec_even, spec_odd = spectrum_of(img.at[u], left_ref, right_ref)
@@ -263,10 +267,6 @@
         own[look, p, 1, :, :quarter] = spec_even[:, quarter:]
         own[look, p, 1, :, quarter:] = spec_odd[:, quarter:]
         energy[look] += w_ref[p] * squares_of(spec_even, spec_odd)
-
-        @pl.when(u > 0)
-        def _():
-            send(u - 1)
 
         return carry
 
@@ -327,7 +327,7 @@
 
     def ring_pairs():
         ahead = lax.rem(me + 1, nlook)
-        first_look = jnp.where(ahead < half, 1, 0)
+        first_look = jnp.where(jnp.logical_and(ahead < half, ahead != 0), 1, 0)
         for look in (first_look, 1 - first_look):
             for p in range(patches):
                 to_near(look, p).wait_recv()
@@ -375,7 +375,7 @@
     turned[...] = summed(PAIRS).astype(jnp.bfloat16)
     for look in range(looks):
         for lag in range(4):
-            factor_ref[look, lag] = jnp.broadcast_to(factor(look, lag), (1, WIN))
+            factor_ref[look, lag : lag + 1, :] = jnp.broadcast_to(factor(look, lag), (1, WIN))
     finish(0)
     returned().start()
 
@@ -439,7 +439,7 @@
         out_specs=[vmem, vmem],
         out_shape=[
             jax.ShapeDtypeStruct((looks, 4, rows, WIN), jnp.float32),
-            jax.ShapeDtypeStruct((looks, 4, 1, WIN), jnp.float32),
+            jax.ShapeDtypeStruct((looks, 4, WIN), jnp.float32),
         ],
         scratch_shapes=[
             pltpu.VMEM(left.shape, jnp.bfloat16),
@@ -485,7 +485,7 @@
         ),
         name="autofocus",
     )(patch_weight, pair_mask, images, left, right, first, second)
-    return surfaces * factors
+    return surfaces * factors[:, :, None, :]
 
 
 def solution(mesh):

time: 82.3 us -> 80.6 us (0.979)
  no operation moved by 1% of the time
where the time goes in v5:
time: 80.6 us; the launch traced here: 80.5 us
  Pallas kernels  78.2 us (97%)
  other arithmetic  2.28 us (3%)
    pallas_call x1, Pallas kernels, per_device(): pl.pallas_call(functools.partial(kernel, nlook, nswath), in_specs=[smem,...  78.2 us
    mul x1, other arithmetic, per_device(): return surfaces * factors[:, :, None, :]  2.28 us

profile of v5, /device:TPU:13, one launch (start us, length us, event | category | flops | bytes accessed | tf_op | source)
XLA Modules:
  0.0 80.5 jit_solution(9270501230113096736)
XLA Ops:
  0.0 78.2 %autofocus.1 = (f32[2,4,128,256]{3,2,1,0:T(8,128)}, f32[2,4,256]{2,1,0:T(4,128)}) custom-call(f32[4]{0:T(128)} %w_ref.1, s32[2,4]{1,0:T(2,128)} %mask_ref.1, bf16[2,4,2,512,512]{4,3,2,1,0:T(8,128)(2,1)} %img_ref.1, bf16[2,256,512]{2,1,0:T(8,128)(2,1)} %constant.8.clone.left_hbm, bf16[2,512,256]{2,1,0:T(8,128)(2,1)} %constant.9.clone.right_hbm, ...), custom_call_target="tpu_custom_call" | custom-call | tf_op jit(solution)/shard_map/autofocus/pallas_call | solution.py:436
  78.2 2.3 %broadcast_multiply_fusion = f32[2,4,128,256]{3,2,1,0:T(8,128)} fusion(f32[2,4,128,256]{3,2,1,0:T(8,128)} %get-tuple-element.7, f32[2,4,256]{2,1,0:T(4,128)} %get-tuple-element.8), kind=kLoop, calls=%fused_computation | loop fusion | flops 262144 | bytes 2105344 | tf_op jit(solution)/shard_map/mul | solution.py:488

commit v6 on v5

--- a/solution.py
+++ b/solution.py
@@ -325,7 +325,12 @@
 
     late = jnp.logical_and(odd, jnp.logical_not(crossing))
 
-    def ring_pairs():
+    def far_pair():
+        for p in range(patches):
+            to_far(p).wait_recv()
+        pair(5, 1, far)
+
+    def ring_pairs(with_far):
         ahead = lax.rem(me + 1, nlook)
         first_look = jnp.where(jnp.logical_and(ahead < half, ahead != 0), 1, 0)
         for look in (first_look, 1 - first_look):
@@ -338,9 +343,11 @@
 
             pair(1 + look, 0, near.at[look])
             pair(3 + look, 1, near.at[look])
+            if with_far and look is first_look:
+                far_pair()
     @pl.when(jnp.logical_not(late))
     def _():
-        ring_pairs()
+        ring_pairs(False)
 
     for p in range(patches):
         to_opp(p).wait_recv()
@@ -381,11 +388,12 @@
 
     @pl.when(late)
     def _():
-        ring_pairs()
-
-    for p in range(patches):
-        to_far(p).wait_recv()
-    pair(5, 1, far)
+        ring_pairs(True)
+
+    @pl.when(jnp.logical_not(late))
+    def _():
+        far_pair()
+
     finish(1)
     finish(3)
     kept = summed(PAIRS - 1)

time: 80.6 us -> 82.7 us (1.026)
  Pallas kernels: 78.2 us -> 80.2 us
    pallas_call x1, Pallas kernels: 78.2 us -> 80.2 us  [per_device(): pl.pallas_call(functools.partial(kernel, nlook, nswath), in_specs=[smem,...]
where the time goes in v6:
time: 82.7 us; the launch traced here: 82.5 us
  Pallas kernels  80.2 us (97%)
  other arithmetic  2.28 us (3%)
    pallas_call x1, Pallas kernels, per_device(): pl.pallas_call(functools.partial(kernel, nlook, nswath), in_specs=[smem,...  80.2 us
    mul x1, other arithmetic, per_device(): return surfaces * factors[:, :, None, :]  2.28 us

profile of v6, /device:TPU:13, one launch (start us, length us, event | category | flops | bytes accessed | tf_op | source)
XLA Modules:
  0.0 82.5 jit_solution(3277355561324053012)
XLA Ops:
  0.0 80.2 %autofocus.1 = (f32[2,4,128,256]{3,2,1,0:T(8,128)}, f32[2,4,256]{2,1,0:T(4,128)}) custom-call(f32[4]{0:T(128)} %w_ref.1, s32[2,4]{1,0:T(2,128)} %mask_ref.1, bf16[2,4,2,512,512]{4,3,2,1,0:T(8,128)(2,1)} %img_ref.1, bf16[2,256,512]{2,1,0:T(8,128)(2,1)} %constant.8.clone.left_hbm, bf16[2,512,256]{2,1,0:T(8,128)(2,1)} %constant.9.clone.right_hbm, ...), custom_call_target="tpu_custom_call" | custom-call | tf_op jit(solution)/shard_map/autofocus/pallas_call | solution.py:444
  80.2 2.3 %broadcast_multiply_fusion = f32[2,4,128,256]{3,2,1,0:T(8,128)} fusion(f32[2,4,128,256]{3,2,1,0:T(8,128)} %get-tuple-element.7, f32[2,4,256]{2,1,0:T(4,128)} %get-tuple-element.8), kind=kLoop, calls=%fused_computation | loop fusion | flops 262144 | bytes 2105344 | tf_op jit(solution)/shard_map/mul | solution.py:496
